TPU v7x, 32 devices: a whole 2x2x4 slice. The times are simulated.
32 devices in a mesh: row: 8 (over z, x), col: 4 (over y, core).
Axes of the slice: x: 2, y: 2, z: 4, core: 2. Of those that a mesh axis runs over, the one named last changes fastest.
Arguments:
- momentum: bfloat16 [16384, 16384], P('row', 'col'), may hold values from -16 to 16
- gradient: bfloat16 [16384, 16384], P('row', 'col'), may hold values from -6 to 6
- right_basis: bfloat16 [1024, 16384], P('row', 'col'), may hold values from -1 to 1
Outputs:
- momentum_next: bfloat16 [16384, 16384], P('row', 'col')
- basis_next: float32 [1024, 16384], P('row', 'col')
- update: bfloat16 [16384, 16384], P('row', 'col')
All inputs are finite; a program needn't handle non-finite values.
Results may differ from a plain program's by a relative error of at most 0.02.
Values may be sent and summed in bfloat16 or wider, within the bound.
A program may use at most 128 MiB of HBM per device.

v0:
```python
import math
import jax
import jax.numpy as jnp
from jax import lax
from jax.sharding import PartitionSpec as P

D = 16384
RANK = 1024
momentum_decay = 0.95
epsilon = 1e-06


def orthonormalize(projected, gram_matrix):
    lower_factor = jnp.linalg.cholesky(gram_matrix)
    solved = jax.scipy.linalg.solve_triangular(lower_factor, projected.T, lower=True)
    return solved.T.astype(jnp.bfloat16)


def self_gram(projected):
    return lax.dot_general(
        projected, projected, (((0,), (0,)), ((), ())), precision=lax.Precision.HIGHEST
    )


def body(momentum, gradient, right_basis):
    buffer = (momentum.astype(jnp.float32) + gradient.astype(jnp.float32)).astype(jnp.bfloat16)
    rank_rows = right_basis.shape[0]
    partial_value = lax.dot_general(
        buffer,
        lax.all_gather(right_basis, "row", axis=0, tiled=True),
        (((1,), (1,)), ((), ())),
        preferred_element_type=jnp.float32,
    )
    row_share = lax.psum_scatter(
        partial_value.astype(jnp.bfloat16), "col", scatter_dimension=0, tiled=True
    ).astype(jnp.float32)
    gram_matrix = lax.psum(self_gram(row_share), ("row", "col"))
    ortho_share = orthonormalize(row_share, gram_matrix)
    orthonormal = lax.all_gather(ortho_share, "col", axis=0, tiled=True)
    right_share = lax.psum_scatter(
        lax.dot_general(
            orthonormal, buffer, (((0,), (0,)), ((), ())), preferred_element_type=jnp.float32
        ).astype(jnp.bfloat16),
        "row",
        scatter_dimension=0,
        tiled=True,
    )
    right_wide = right_share.astype(jnp.float32)
    gathered = lax.all_gather(right_share, "row", axis=0, tiled=True)
    gathered_wide = gathered.astype(jnp.float32)
    sums_total = lax.psum(jnp.sum(gathered_wide * gathered_wide, axis=1), "col")
    inverse_norm = lax.rsqrt(sums_total + epsilon)[:, None]
    scaled = (gathered_wide * inverse_norm).astype(jnp.bfloat16)
    feedback = jnp.dot(orthonormal, gathered, preferred_element_type=jnp.float32)
    direction = jnp.dot(orthonormal, scaled, preferred_element_type=jnp.float32)
    offset = lax.axis_index("row") * rank_rows
    basis_next = right_wide * lax.dynamic_slice_in_dim(inverse_norm, offset, rank_rows, 0)
    momentum_next = (buffer.astype(jnp.float32) - (1.0 - momentum_decay) * feedback).astype(
        jnp.bfloat16
    )
    update_scale = D / math.sqrt(RANK)
    update = (update_scale * direction).astype(jnp.bfloat16)
    return (momentum_next, basis_next, update)


def solution(mesh):
    return jax.shard_map(
        body,
        mesh=mesh,
        in_specs=(P("row", "col"), P("row", "col"), P("row", "col")),
        out_specs=(P("row", "col"), P("row", "col"), P("row", "col")),
        check_vma=False,
    )
```

profile of v0, /device:TPU:0, one launch (start us, length us, event | category | flops | bytes accessed | tf_op | source)
XLA Modules:
  0.0 1132.3 jit_solution(6209591932826324028)
XLA Ops:
  7.9 129.4 %all-gather.4.cloned.1.call-done = bf16[1024,4096]{1,0:T(8,128)(2,1)} async-done(((bf16[128,4096]{1,0:T(8,128)(2,1)}), bf16[1024,4096]{1,0:T(8,128)(2,1)}) %all-gather.4.cloned.1.call-update) | async-done | bytes 8388624 | tf_op jit(solution)/shard_map/all_gather | solution.py:30
  137.3 25.8 %convolution_convert_fusion.1 = bf16[2048,1024]{1,0:T(8,128)(2,1)} fusion(bf16[1024,4096]{1,0:T(8,128)(2,1)} %all-gather.4.cloned.1.call-done, bf16[2048,4096]{1,0:T(8,128)(2,1)} %param.4, bf16[2048,4096]{1,0:T(8,128)(2,1)} %param.3), kind=kOutput, calls=%fused_computation.15 | convolution fusion | flops 17215520768 | bytes 46137344 | tf_op jit(solution)/shard_map/dot_general | solution.py:28
  163.2 42.9 %reduce-scatter.3.cloned.1.call-done = bf16[512,1024]{1,0:T(8,128)(2,1)} async-done(((bf16[2048,1024]{1,0:T(8,128)(2,1)}), bf16[512,1024]{1,0:T(8,128)(2,1)}) %reduce-scatter.3.cloned.1.call-update) | async-done | bytes 1048592 | tf_op jit(solution)/shard_map/reduce_scatter | solution.py:34
  211.3 143.2 %all-reduce.3.cloned.1.call-done = f32[1024,1024]{0,1:T(8,128)} async-done(((f32[1024,1024]{0,1:T(8,128)}), f32[1024,1024]{0,1:T(8,128)}) %all-reduce.3.cloned.1.call-update) | async-done | bytes 4194320 | tf_op jit(solution)/shard_map/psum | solution.py:37
  366.5 11.7 %cholesky.223 = f32[128,128]{1,0:T(8,128)S(1)} custom-call(f32[128,128]{1,0:T(8,128)S(1)} %cholesky.580), custom_call_target="Cholesky" | custom-call | tf_op jit(solution)/shard_map/jit(cholesky)/cholesky | solution.py:14
  378.2 9.8 custom-call.63
  395.2 12.1 %cholesky.244 = f32[128,128]{1,0:T(8,128)S(1)} custom-call(f32[128,128]{1,0:T(8,128)S(1)} %cholesky.584), custom_call_target="Cholesky" | custom-call | tf_op jit(solution)/shard_map/jit(cholesky)/cholesky | solution.py:14
  422.7 13.2 %cholesky.468 = f32[128,128]{1,0:T(8,128)} custom-call(f32[128,128]{1,0:T(8,128)} %cholesky.589), custom_call_target="Cholesky" | custom-call | tf_op jit(solution)/shard_map/jit(cholesky)/cholesky | solution.py:14
  438.0 11.3 custom-call.65
  453.6 12.5 %cholesky.487 = f32[128,128]{1,0:T(8,128)} custom-call(f32[128,128]{1,0:T(8,128)S(1)} %cholesky.594), custom_call_target="Cholesky" | custom-call | tf_op jit(solution)/shard_map/jit(cholesky)/cholesky | solution.py:14
  468.2 10.4 custom-call.66
  482.9 11.7 %cholesky.506 = f32[128,128]{1,0:T(8,128)S(1)} custom-call(f32[128,128]{1,0:T(8,128)S(1)} %cholesky.599), custom_call_target="Cholesky" | custom-call | tf_op jit(solution)/shard_map/jit(cholesky)/cholesky | solution.py:14
  495.9 10.0 custom-call.67
  509.2 11.7 %cholesky.526 = f32[128,128]{1,0:T(8,128)S(1)} custom-call(f32[128,128]{1,0:T(8,128)S(1)} %cholesky.604), custom_call_target="Cholesky" | custom-call | tf_op jit(solution)/shard_map/jit(cholesky)/cholesky | solution.py:14
  535.0 12.0 %cholesky.546 = f32[128,128]{1,0:T(8,128)S(1)} custom-call(f32[128,128]{1,0:T(8,128)S(1)} %cholesky.609), custom_call_target="Cholesky" | custom-call | tf_op jit(solution)/shard_map/jit(cholesky)/cholesky | solution.py:14
  560.9 11.7 %cholesky.564 = f32[128,128]{1,0:T(8,128)S(1)} custom-call(f32[128,128]{1,0:T(8,128)S(1)} %convolution_subtract_fusion.13), custom_call_target="Cholesky" | custom-call | tf_op jit(solution)/shard_map/jit(cholesky)/cholesky | solution.py:14
  584.4 29.0 %while.1 = (s32[]{:T(128)}, f32[1024,1024]{1,0:T(8,128)}, s32[8,2]{0,1:T(2,128)S(1)}, f32[8,128,128]{2,1,0:T(8,128)}, s32[]{:T(128)}) while((s32[]{:T(128)}, f32[1024,1024]{1,0:T(8,128)}, s32[8,2]{0,1:T(2,128)S(1)}, f32[8,128,128]{2,1,0:T(8,128)}, s32[]{:T(128)}) %tuple.57), condition=%wide.while_cond, body=%wide.while_body.sunk | while | flops 2 | bytes 132205 | solution.py:15
  613.4 80.2 %custom-call.70 = f32[8,128,128]{1,2,0:T(8,128)} custom-call(f32[8,128,128]{2,1,0:T(8,128)} %get-tuple-element.10), custom_call_target="InvertDiagBlocksLowerTriangular" | custom-call | tf_op jit(solution)/shard_map/jit(_solve_triangular)/triangular_solve | solution.py:15
  724.2 33.9 %all-gather.6.cloned.1.call-done = bf16[2048,1024]{0,1:T(8,128)(2,1)} async-done(((bf16[512,1024]{0,1:T(8,128)(2,1)}), bf16[2048,1024]{0,1:T(8,128)(2,1)}) %all-gather.6.cloned.1.call-update) | async-done | bytes 4194320 | tf_op jit(solution)/shard_map/all_gather | solution.py:39
  758.1 24.2 %convolution_convert_fusion = bf16[1024,4096]{1,0:T(8,128)(2,1)} fusion(bf16[2048,1024]{0,1:T(8,128)(2,1)} %all-gather.6.cloned.1.call-done, bf16[2048,4096]{1,0:T(8,128)(2,1)} %param.4, bf16[2048,4096]{1,0:T(8,128)(2,1)} %param.3), kind=kOutput, calls=%fused_computation.10 | convolution fusion | flops 17217617920 | bytes 46137344 | tf_op jit(solution)/shard_map/dot_general | solution.py:41
  782.3 147.5 %reduce-scatter.5.cloned.1.call-done = bf16[128,4096]{1,0:T(8,128)(2,1)} async-done(((bf16[1024,4096]{1,0:T(8,128)(2,1)}), bf16[128,4096]{1,0:T(8,128)(2,1)}) %reduce-scatter.5.cloned.1.call-update) | async-done | bytes 1048592 | tf_op jit(solution)/shard_map/reduce_scatter | solution.py:40
  929.9 125.6 %all-gather.8.cloned.1.call-done = bf16[1024,4096]{1,0:T(8,128)(2,1)} async-done(((bf16[128,4096]{1,0:T(8,128)(2,1)}), bf16[1024,4096]{1,0:T(8,128)(2,1)}) %all-gather.8.cloned.1.call-update) | async-done | bytes 8388624 | tf_op jit(solution)/shard_map/all_gather | solution.py:49
  1066.5 26.4 %multiply_convert_fusion = bf16[2048,4096]{1,0:T(8,128)(2,1)} fusion(bf16[2048,1024]{0,1:T(8,128)(2,1)} %all-gather.6.cloned.1.call-done, bf16[1024,4096]{1,0:T(8,128)(2,1)} %all-gather.8.cloned.1.call-done, f32[1024]{0:T(1024)S(1)} %add_rsqrt_fusion), kind=kOutput, calls=%fused_computation.2 | convolution fusion | flops 17209229312 | bytes 29364224 | tf_op jit(solution)/shard_map/dot_general | solution.py:55
  1092.9 30.5 %subtract_convert_fusion = bf16[2048,4096]{1,0:T(8,128)(2,1)} fusion(bf16[2048,1024]{0,1:T(8,128)(2,1)S(1)} %copy-done.5, bf16[1024,4096]{1,0:T(8,128)(2,1)} %all-gather.8.cloned.1.call-done, bf16[2048,4096]{1,0:T(8,128)(2,1)} %param.4, bf16[2048,4096]{1,0:T(8,128)(2,1)} %param.3), kind=kOutput, calls=%fused_computation.3 | convolution fusion | flops 17246978048 | bytes 62914560 | tf_op jit(solution)/shard_map/dot_general | solution.py:54
  (123 shorter events, 164.9 us)
Async XLA Ops:
  7.2 130.2 %all-gather.4.cloned.1.call-start = ((), (), s32[]{:S(2)}) async-start(), calls=%async_computation.2 | async-start | bytes 9437184 | tf_op jit(solution)/shard_map/all_gather | solution.py:30
  7.9 198.2 %reduce-scatter.3.cloned.1.call-start = ((), (), s32[]{:S(2)}) async-start(), calls=%async_computation.3 | async-start | bytes 5242880 | tf_op jit(solution)/shard_map/reduce_scatter | solution.py:34
  163.1 191.4 %all-reduce.3.cloned.1.call-start = ((), (), s32[]{:S(2)}) async-start(), calls=%async_computation.4 | async-start | bytes 8388608 | tf_op jit(solution)/shard_map/psum | solution.py:37
  206.1 5.0 copy-start
  211.0 547.1 %all-gather.6.cloned.1.call-start = ((), (), s32[]{:S(2)}) async-start(), calls=%async_computation.5 | async-start | bytes 5242880 | tf_op jit(solution)/shard_map/all_gather | solution.py:39
  364.5 2.0 copy-start.1
  394.5 0.8 copy-start.3
  693.6 7.2 copy-start.4
  724.2 205.7 %reduce-scatter.5.cloned.1.call-start = ((), (), s32[]{:S(2)}) async-start(), calls=%async_computation.6 | async-start | bytes 9437184 | tf_op jit(solution)/shard_map/reduce_scatter | solution.py:40
  782.3 273.2 %all-gather.8.cloned.1.call-start = ((), (), s32[]{:S(2)}) async-start(), calls=%async_computation.7 | async-start | bytes 9437184 | tf_op jit(solution)/shard_map/all_gather | solution.py:49
  1066.5 26.4 %copy-start.5 = (bf16[2048,1024]{0,1:T(8,128)(2,1)S(1)}, bf16[2048,1024]{0,1:T(8,128)(2,1)}, u32[]{:S(2)}) copy-start(bf16[2048,1024]{0,1:T(8,128)(2,1)} %all-gather.6.cloned.1.call-done) | copy-start | bytes 12582916
  1092.9 30.5 %copy-start.2 = (bf16[128,4096]{1,0:T(8,128)(2,1)S(1)}, bf16[128,4096]{1,0:T(8,128)(2,1)}, u32[]{:S(2)}) copy-start(bf16[128,4096]{1,0:T(8,128)(2,1)} %reduce-scatter.5.cloned.1.call-done) | copy-start | bytes 3145732
Sparse Core Ops, SparseCore 0:
  10.1 127.1 all-gather.3
  163.3 42.7 reduce-scatter.2
  212.2 142.2 all-reduce.2
  724.3 33.7 all-gather.5
  782.4 147.4 reduce-scatter.4
  931.9 123.5 all-gather.7
where the time goes:
time: 1140 us; the launch traced here: 1130 us
  waiting for transfers between devices  623 us (55%)
  other arithmetic  275 us (24%)
  matrix products  167 us (15%)
  local copies, waits for them, and re-layouts  41.1 us (4%)
  between operations  19.9 us (2%)
    another operation x30, other arithmetic, orthonormalize(): lower_factor = jnp.linalg.cholesky(gram_matrix)  178 us
    reduce_scatter x1, waiting for transfers between devices, body(): lax.psum_scatter(lax.dot_general(orthonormal, buffer, (((0,), (0,)), ((),...  148 us
    psum x1, waiting for transfers between devices, body(): gram_matrix = lax.psum(self_gram(row_share), ('row', 'col'))  143 us
    all_gather x1, waiting for transfers between devices, body(): lax.all_gather(right_basis, 'row', axis=0, tiled=True)  129 us
    all_gather x1, waiting for transfers between devices, body(): gathered = lax.all_gather(right_share, 'row', axis=0, tiled=True)  126 us
    another operation x3, other arithmetic, orthonormalize(): jax.scipy.linalg.solve_triangular(lower_factor, projected.T, lower=True)  85.1 us
    reduce_scatter x1, waiting for transfers between devices, body(): lax.psum_scatter(partial_value.astype(jnp.bfloat16), 'col', scatter_dimen...  42.9 us
    all_gather x1, waiting for transfers between devices, body(): orthonormal = lax.all_gather(ortho_share, 'col', axis=0, tiled=True)  33.9 us
  transfers between devices with their start and end apart: 6, of which 6 were waited for; matrix products, arithmetic and copies ran while one was open for 0% of the time, Pallas kernels for 0%

commit v1 on v0

--- a/solution.py
+++ b/solution.py
@@ -46,7 +46,25 @@
         tiled=True,
     )
     right_wide = right_share.astype(jnp.float32)
-    gathered = lax.all_gather(right_share, "row", axis=0, tiled=True)
+    length, index, rows = (lax.axis_size("row"), lax.axis_index("row"), right_share.shape[0])
+    right = [(i, (i + 1) % length) for i in range(length)]
+    left = [(i, (i - 1) % length) for i in range(length)]
+    gathered = jnp.zeros(
+        (*right_share.shape[:0], length * rows, *right_share.shape[0 + 1 :]), right_share.dtype
+    )
+    gathered = lax.dynamic_update_slice_in_dim(gathered, right_share, index * rows, axis=0)
+    from_left = from_right = right_share
+    half = length // 2
+    for step in range(1, half + 1):
+        from_left = lax.ppermute(from_left, "row", right)
+        gathered = lax.dynamic_update_slice_in_dim(
+            gathered, from_left, (index - step) % length * rows, axis=0
+        )
+        if step < length - half:
+            from_right = lax.ppermute(from_right, "row", left)
+            gathered = lax.dynamic_update_slice_in_dim(
+                gathered, from_right, (index + step) % length * rows, axis=0
+            )
     gathered_wide = gathered.astype(jnp.float32)
     sums_total = lax.psum(jnp.sum(gathered_wide * gathered_wide, axis=1), "col")
     inverse_norm = lax.rsqrt(sums_total + epsilon)[:, None]

time: 1140 us -> 1180 us (1.035)
  waiting for transfers between devices: 623 us -> 645 us
  starting transfers between devices: 0.24 us -> 16.9 us
    ppermute x0 -> x7, waiting for transfers between devices: none -> 146 us  [the longest x4 146 us: body(): from_left = lax.ppermute(from_left, 'row', right)]
    all_gather x1 -> x0, waiting for transfers between devices: 126 us -> none  [body(): gathered = lax.all_gather(right_share, 'row', axis=0, tiled=True)]
    ppermute x0 -> x7, starting transfers between devices: none -> 16.7 us  [the longest x4 8.83 us: body(): from_left = lax.ppermute(from_left, 'row', right)]
  transfers between devices with their start and end apart: 6 -> 12, of which waited for: 6 -> 10; matrix products, arithmetic and copies ran while one was open for 0% -> 0% of each run, Pallas kernels for 0% -> 0%
where the time goes in v1:
time: 1180 us; the launch traced here: 1170 us
  waiting for transfers between devices  645 us (55%)
  other arithmetic  271 us (23%)
  matrix products  168 us (14%)
  local copies, waits for them, and re-layouts  47.7 us (4%)
  between operations  19.4 us (2%)
  starting transfers between devices  16.9 us (1%)
    another operation x30, other arithmetic, orthonormalize(): lower_factor = jnp.linalg.cholesky(gram_matrix)  178 us
    reduce_scatter x1, waiting for transfers between devices, body(): lax.psum_scatter(lax.dot_general(orthonormal, buffer, (((0,), (0,)), ((),...  148 us
    ppermute x4, waiting for transfers between devices, body(): from_left = lax.ppermute(from_left, 'row', right)  146 us
    psum x1, waiting for transfers between devices, body(): gram_matrix = lax.psum(self_gram(row_share), ('row', 'col'))  143 us
    all_gather x1, waiting for transfers between devices, body(): lax.all_gather(right_basis, 'row', axis=0, tiled=True)  129 us
    another operation x3, other arithmetic, orthonormalize(): jax.scipy.linalg.solve_triangular(lower_factor, projected.T, lower=True)  85.1 us
    reduce_scatter x1, waiting for transfers between devices, body(): lax.psum_scatter(partial_value.astype(jnp.bfloat16), 'col', scatter_dimen...  42.9 us
    all_gather x1, waiting for transfers between devices, body(): orthonormal = lax.all_gather(ortho_share, 'col', axis=0, tiled=True)  33.9 us
  transfers between devices with their start and end apart: 12, of which 10 were waited for; matrix products, arithmetic and copies ran while one was open for 0% of the time, Pallas kernels for 0%

profile of v1, /device:TPU:0, one launch (start us, length us, event | category | flops | bytes accessed | tf_op | source)
XLA Modules:
  0.0 1173.1 jit_solution(13412257922681826083)
XLA Ops:
  7.9 129.4 %all-gather.3.cloned.1.call-done = bf16[1024,4096]{1,0:T(8,128)(2,1)} async-done(((bf16[128,4096]{1,0:T(8,128)(2,1)}), bf16[1024,4096]{1,0:T(8,128)(2,1)}) %all-gather.3.cloned.1.call-update) | async-done | bytes 8388624 | tf_op jit(solution)/shard_map/all_gather | solution.py:30
  137.3 25.8 %convolution_convert_fusion.1 = bf16[2048,1024]{1,0:T(8,128)(2,1)} fusion(bf16[1024,4096]{1,0:T(8,128)(2,1)} %all-gather.3.cloned.1.call-done, bf16[2048,4096]{1,0:T(8,128)(2,1)} %param.4, bf16[2048,4096]{1,0:T(8,128)(2,1)} %param.3), kind=kOutput, calls=%fused_computation.15 | convolution fusion | flops 17215520768 | bytes 46137344 | tf_op jit(solution)/shard_map/dot_general | solution.py:28
  163.2 42.9 %reduce-scatter.3.cloned.1.call-done = bf16[512,1024]{1,0:T(8,128)(2,1)} async-done(((bf16[2048,1024]{1,0:T(8,128)(2,1)}), bf16[512,1024]{1,0:T(8,128)(2,1)}) %reduce-scatter.3.cloned.1.call-update) | async-done | bytes 1048592 | tf_op jit(solution)/shard_map/reduce_scatter | solution.py:34
  211.3 143.3 %all-reduce.3.cloned.1.call-done = f32[1024,1024]{0,1:T(8,128)} async-done(((f32[1024,1024]{0,1:T(8,128)}), f32[1024,1024]{0,1:T(8,128)}) %all-reduce.3.cloned.1.call-update) | async-done | bytes 4194320 | tf_op jit(solution)/shard_map/psum | solution.py:37
  366.9 11.7 cholesky.223
  395.7 11.9 %cholesky.244 = f32[128,128]{1,0:T(8,128)S(1)} custom-call(f32[128,128]{1,0:T(8,128)S(1)} %cholesky.584), custom_call_target="Cholesky" | custom-call | tf_op jit(solution)/shard_map/jit(cholesky)/cholesky | solution.py:14
  422.9 13.2 %cholesky.468 = f32[128,128]{1,0:T(8,128)} custom-call(f32[128,128]{1,0:T(8,128)} %cholesky.589), custom_call_target="Cholesky" | custom-call | tf_op jit(solution)/shard_map/jit(cholesky)/cholesky | solution.py:14
  438.2 11.3 custom-call.65
  453.8 12.5 %cholesky.487 = f32[128,128]{1,0:T(8,128)} custom-call(f32[128,128]{1,0:T(8,128)S(1)} %cholesky.594), custom_call_target="Cholesky" | custom-call | tf_op jit(solution)/shard_map/jit(cholesky)/cholesky | solution.py:14
  483.2 11.7 cholesky.506
  509.6 11.7 cholesky.526
  535.5 11.8 %cholesky.546 = f32[128,128]{1,0:T(8,128)S(1)} custom-call(f32[128,128]{1,0:T(8,128)S(1)} %cholesky.609), custom_call_target="Cholesky" | custom-call | tf_op jit(solution)/shard_map/jit(cholesky)/cholesky | solution.py:14
  561.1 11.7 cholesky.564
  584.6 29.0 %while.1 = (s32[]{:T(128)}, f32[1024,1024]{1,0:T(8,128)}, s32[8,2]{0,1:T(2,128)S(1)}, f32[8,128,128]{2,1,0:T(8,128)}, s32[]{:T(128)}) while((s32[]{:T(128)}, f32[1024,1024]{1,0:T(8,128)}, s32[8,2]{0,1:T(2,128)S(1)}, f32[8,128,128]{2,1,0:T(8,128)}, s32[]{:T(128)}) %tuple.57), condition=%wide.while_cond, body=%wide.while_body.sunk | while | flops 2 | bytes 132205 | solution.py:15
  613.6 80.2 %custom-call.70 = f32[8,128,128]{1,2,0:T(8,128)} custom-call(f32[8,128,128]{2,1,0:T(8,128)} %get-tuple-element.10), custom_call_target="InvertDiagBlocksLowerTriangular" | custom-call | tf_op jit(solution)/shard_map/jit(_solve_triangular)/triangular_solve | solution.py:15
  724.7 33.9 %all-gather.5.cloned.1.call-done = bf16[2048,1024]{0,1:T(8,128)(2,1)} async-done(((bf16[512,1024]{0,1:T(8,128)(2,1)}), bf16[2048,1024]{0,1:T(8,128)(2,1)}) %all-gather.5.cloned.1.call-update) | async-done | bytes 4194320 | tf_op jit(solution)/shard_map/all_gather | solution.py:39
  758.5 24.2 %convolution_convert_fusion = bf16[1024,4096]{1,0:T(8,128)(2,1)} fusion(bf16[2048,1024]{0,1:T(8,128)(2,1)} %all-gather.5.cloned.1.call-done, bf16[2048,4096]{1,0:T(8,128)(2,1)} %param.4, bf16[2048,4096]{1,0:T(8,128)(2,1)} %param.3), kind=kOutput, calls=%fused_computation.10 | convolution fusion | flops 17217617920 | bytes 46137344 | tf_op jit(solution)/shard_map/dot_general | solution.py:41
  782.7 148.0 %reduce-scatter.5.cloned.1.call-done = bf16[128,4096]{1,0:T(8,128)(2,1)} async-done(((bf16[1024,4096]{1,0:T(8,128)(2,1)}), bf16[128,4096]{1,0:T(8,128)(2,1)}) %reduce-scatter.5.cloned.1.call-update) | async-done | bytes 1048592 | tf_op jit(solution)/shard_map/reduce_scatter | solution.py:40
  935.5 41.7 %collective-permute-done = bf16[128,4096]{1,0:T(8,128)(2,1)} collective-permute-done((bf16[128,4096]{1,0:T(8,128)(2,1)}, bf16[128,4096]{1,0:T(8,128)(2,1)}, u32[]{:S(2)}, u32[]{:S(2)}) %collective-permute-start) | collective-permute-done | bytes 1048608 | tf_op jit(solution)/shard_map/ppermute | solution.py:59
  983.0 41.0 %collective-permute-done.2 = bf16[128,4096]{1,0:T(8,128)(2,1)S(1)} collective-permute-done((bf16[128,4096]{1,0:T(8,128)(2,1)}, bf16[128,4096]{1,0:T(8,128)(2,1)S(1)}, u32[]{:S(2)}, u32[]{:S(2)}) %collective-permute-start.2) | collective-permute-done | bytes 1048608 | tf_op jit(solution)/shard_map/ppermute | solution.py:59
  1030.3 40.3 %collective-permute-done.4 = bf16[128,4096]{1,0:T(8,128)(2,1)S(1)} collective-permute-done((bf16[128,4096]{1,0:T(8,128)(2,1)S(1)}, bf16[128,4096]{1,0:T(8,128)(2,1)S(1)}, u32[]{:S(2)}, u32[]{:S(2)}) %collective-permute-start.4) | collective-permute-done | bytes 1048608 | tf_op jit(solution)/shard_map/ppermute | solution.py:59
  1073.6 23.3 %collective-permute-done.6 = bf16[128,4096]{1,0:T(8,128)(2,1)S(1)} collective-permute-done((bf16[128,4096]{1,0:T(8,128)(2,1)S(1)}, bf16[128,4096]{1,0:T(8,128)(2,1)S(1)}, u32[]{:S(2)}, u32[]{:S(2)}) %collective-permute-start.6) | collective-permute-done | bytes 1048608 | tf_op jit(solution)/shard_map/ppermute | solution.py:59
  1107.6 25.4 %multiply_convert_fusion = bf16[2048,4096]{1,0:T(8,128)(2,1)} fusion(bf16[2048,1024]{0,1:T(8,128)(2,1)} %all-gather.5.cloned.1.call-done, bf16[1024,4096]{1,0:T(8,128)(2,1)} %copy-done, f32[1024]{0:T(1024)S(1)} %add_rsqrt_fusion), kind=kOutput, calls=%fused_computation.2 | convolution fusion | flops 17209229312 | bytes 29364224 | tf_op jit(solution)/shard_map/dot_general | solution.py:73
  1133.0 31.7 %subtract_convert_fusion = bf16[2048,4096]{1,0:T(8,128)(2,1)} fusion(bf16[2048,1024]{0,1:T(8,128)(2,1)} %all-gather.5.cloned.1.call-done, bf16[1024,4096]{1,0:T(8,128)(2,1)} %copy-done, bf16[2048,4096]{1,0:T(8,128)(2,1)} %param.4, bf16[2048,4096]{1,0:T(8,128)(2,1)} %param.3), kind=kOutput, calls=%fused_computation.3 | convolution fusion | flops 17246978048 | bytes 62914560 | tf_op jit(solution)/shard_map/dot_general | solution.py:72
  (143 shorter events, 215.3 us)
Async XLA Ops:
  7.2 130.2 %all-gather.3.cloned.1.call-start = ((), (), s32[]{:S(2)}) async-start(), calls=%async_computation.2 | async-start | bytes 9437184 | tf_op jit(solution)/shard_map/all_gather | solution.py:30
  7.9 198.2 %reduce-scatter.3.cloned.1.call-start = ((), (), s32[]{:S(2)}) async-start(), calls=%async_computation.3 | async-start | bytes 5242880 | tf_op jit(solution)/shard_map/reduce_scatter | solution.py:34
  163.1 191.5 %all-reduce.3.cloned.1.call-start = ((), (), s32[]{:S(2)}) async-start(), calls=%async_computation.4 | async-start | bytes 8388608 | tf_op jit(solution)/shard_map/psum | solution.py:37
  206.0 5.0 copy-start.1
  211.0 547.5 %all-gather.5.cloned.1.call-start = ((), (), s32[]{:S(2)}) async-start(), calls=%async_computation.5 | async-start | bytes 5242880 | tf_op jit(solution)/shard_map/all_gather | solution.py:39
  364.9 2.0 copy-start.2
  394.9 0.8 copy-start.4
  693.9 7.3 copy-start.5
  724.6 206.1 %reduce-scatter.5.cloned.1.call-start = ((), (), s32[]{:S(2)}) async-start(), calls=%async_computation.6 | async-start | bytes 9437184 | tf_op jit(solution)/shard_map/reduce_scatter | solution.py:40
  930.7 46.4 %collective-permute-start = (bf16[128,4096]{1,0:T(8,128)(2,1)}, bf16[128,4096]{1,0:T(8,128)(2,1)}, u32[]{:S(2)}, u32[]{:S(2)}) collective-permute-start(bf16[128,4096]{1,0:T(8,128)(2,1)} %reduce-scatter.5.cloned.1.call-done), channel_id=1, source_target_pairs={{0,4},{4,8},{8,12},{12,16},{16,20},{20,24},{24,28},{28,0},{1,5},{5... | collective-permute-start | bytes 3145736 | tf_op jit(solution)/shard_map/ppermute | solution.py:59
  932.2 47.4 %collective-permute-start.1 = (bf16[128,4096]{1,0:T(8,128)(2,1)}, bf16[128,4096]{1,0:T(8,128)(2,1)S(1)}, u32[]{:S(2)}, u32[]{:S(2)}) collective-permute-start(bf16[128,4096]{1,0:T(8,128)(2,1)} %reduce-scatter.5.cloned.1.call-done), channel_id=1, source_target_pairs={{0,28},{4,0},{8,4},{12,8},{16,12},{20,16},{24,20},{28,24},{1,29},{... | collective-permute-start | bytes 3145736 | tf_op jit(solution)/shard_map/ppermute | solution.py:64
  977.1 46.9 %collective-permute-start.2 = (bf16[128,4096]{1,0:T(8,128)(2,1)}, bf16[128,4096]{1,0:T(8,128)(2,1)S(1)}, u32[]{:S(2)}, u32[]{:S(2)}) collective-permute-start(bf16[128,4096]{1,0:T(8,128)(2,1)} %collective-permute-done), channel_id=1, source_target_pairs={{0,4},{4,8},{8,12},{12,16},{16,20},{20,24},{24,28},{28,0},{1,5},{5... | collective-permute-start | bytes 3145736 | tf_op jit(solution)/shard_map/ppermute | solution.py:59
  979.6 3.3 copy-start.3
  979.6 48.2 %collective-permute-start.3 = (bf16[128,4096]{1,0:T(8,128)(2,1)S(1)}, bf16[128,4096]{1,0:T(8,128)(2,1)S(1)}, u32[]{:S(2)}, u32[]{:S(2)}) collective-permute-start(bf16[128,4096]{1,0:T(8,128)(2,1)S(1)} %collective-permute-done.1), channel_id=1, source_target_pairs={{0,28},{4,0},{8,4},{12,8},{16,12},{20,16},{24,20},{28,24},{1,29},{... | collective-permute-start | bytes 3145736 | tf_op jit(solution)/shard_map/ppermute | solution.py:64
  1024.0 46.7 %collective-permute-start.4 = (bf16[128,4096]{1,0:T(8,128)(2,1)S(1)}, bf16[128,4096]{1,0:T(8,128)(2,1)S(1)}, u32[]{:S(2)}, u32[]{:S(2)}) collective-permute-start(bf16[128,4096]{1,0:T(8,128)(2,1)S(1)} %collective-permute-done.2), channel_id=1, source_target_pairs={{0,4},{4,8},{8,12},{12,16},{16,20},{20,24},{24,28},{28,0},{1,5},{5... | collective-permute-start | bytes 3145736 | tf_op jit(solution)/shard_map/ppermute | solution.py:59
  1027.8 45.6 %collective-permute-start.5 = (bf16[128,4096]{1,0:T(8,128)(2,1)S(1)}, bf16[128,4096]{1,0:T(8,128)(2,1)S(1)}, u32[]{:S(2)}, u32[]{:S(2)}) collective-permute-start(bf16[128,4096]{1,0:T(8,128)(2,1)S(1)} %collective-permute-done.3), channel_id=1, source_target_pairs={{0,28},{4,0},{8,4},{12,8},{16,12},{20,16},{24,20},{28,24},{1,29},{... | collective-permute-start | bytes 3145736 | tf_op jit(solution)/shard_map/ppermute | solution.py:64
  1070.7 26.2 %collective-permute-start.6 = (bf16[128,4096]{1,0:T(8,128)(2,1)S(1)}, bf16[128,4096]{1,0:T(8,128)(2,1)S(1)}, u32[]{:S(2)}, u32[]{:S(2)}) collective-permute-start(bf16[128,4096]{1,0:T(8,128)(2,1)S(1)} %collective-permute-done.4), channel_id=1, source_target_pairs={{0,4},{4,8},{8,12},{12,16},{16,20},{20,24},{24,28},{28,0},{1,5},{5... | collective-permute-start | bytes 3145736 | tf_op jit(solution)/shard_map/ppermute | solution.py:59
  1097.0 3.2 copy-start
Sparse Core Ops, SparseCore 0:
  10.1 127.1 all-gather.2
  163.3 42.7 reduce-scatter.2
  212.2 142.4 all-reduce.2
  724.7 33.7 all-gather.4
  782.8 147.8 reduce-scatter.4
